TPU v7x, 256 devices: a whole 4x4x8 slice. The times are simulated.
256 devices in a mesh: dp: 128 (over y_hi, x, z, core), pipe: 2 (over y_lo).
Axes of the slice: x: 4, y: 4 (y_hi: 2, y_lo: 2; y = y_hi * 2 + y_lo), z: 8, core: 2. Of those that a mesh axis runs over, the one named last changes fastest.
Arguments:
- block_input: bfloat16 [2, 32768, 1536], P('pipe', 'dp'), may hold values from -100 to 100
- saved_qkv: bfloat16 [2, 32768, 4608], P('pipe', 'dp'), may hold values from -10 to 10
- cotangent: bfloat16 [2, 32768, 1536], P('pipe', 'dp'), may hold values from -6 to 6
- mod_table: float32 [2, 3, 1536], P('pipe'), may hold values from -3 to 3
- clip_condition: float32 [2, 1024, 4608], P('pipe', 'dp'), may hold values from -3 to 3
- clip_frames: int32 [2, 1024], P('pipe', 'dp'), may hold values from 0 to 8, as said below
- frame_tokens: int32 [2, 1024], P('pipe', 'dp'), may hold values from 2 to 64, as said below
- tile_layout: int32 [2, 256, 2], P('pipe', 'dp'), may hold values from 0 to 1, as said below
- frozen_qkv: bfloat16 [2, 1536, 4608], P('pipe', 'dp'), may hold values from -0.15625 to 0.15625
- frozen_out: bfloat16 [2, 1536, 1536], P('pipe', 'dp'), may hold values from -0.15625 to 0.15625
- adapters: bfloat16 [2, 9216, 128], P('pipe'), may hold values from -0.15625 to 0.15625
Outputs:
- upstream: bfloat16 [2, 32768, 1536], P('pipe', 'dp')
- d_table: float32 [2, 3, 1536], P('pipe')
- d_adapters: float32 [2, 9216, 128], P('pipe', 'dp')
Inputs may be any that keep to these rules, and one draw needn't show every extreme that they name: `clip_frames`: clips are packed in slot order; a slot with 0 frames holds no clip and so does every later slot of that device; the clips of one device hold at most 256 tokens. `frame_tokens`: even. `tile_layout`: every diagonal tile is live.
All inputs are finite; a program needn't handle non-finite values.
Results may differ from a plain program's by a relative error of at most 0.0065.
Values may be sent and summed in bfloat16 or wider, within the bound.
A program may use at most 128 MiB of HBM per device.

v0:
```python
import jax
import jax.numpy as jnp
from jax import lax
from jax.sharding import PartitionSpec as P

HEAD = 128
TILE = 128


EPSILON = 1e-06
HIGH = lax.Precision.HIGHEST


def passed_along(block, axis, distance):
    devices = range(lax.axis_size(axis))
    route = [((i - distance) % len(devices), i) for i in devices]
    return lax.ppermute(block, axis, route)


def contract_last(left, right):
    return lax.dot_general(
        left, right, (((1,), (1,)), ((), ())), preferred_element_type=jnp.float32
    )


def contract_first(left, right):
    return lax.dot_general(
        left, right, (((0,), (0,)), ((), ())), preferred_element_type=jnp.float32
    )


def on_device(
    block_input,
    saved_qkv,
    cotangent,
    mod_table,
    clip_condition,
    clip_frames,
    frame_tokens,
    tile_layout,
    frozen_qkv,
    frozen_out,
    adapters,
):
    tokens_here = block_input[0]
    rows, width = tokens_here.shape
    saved = saved_qkv[0]
    inner = saved.shape[1] // 3
    heads = inner // HEAD
    slots = clip_frames.shape[1]
    tiles = tile_layout.shape[1]
    adapter_rows = adapters[0]
    down_qkv = adapter_rows[:width]
    up_qkv = adapter_rows[width : width + 3 * inner]
    down_out = adapter_rows[width + 3 * inner : width + 4 * inner]
    up_out = adapter_rows[width + 4 * inner :]
    clip_ends = jnp.cumsum(clip_frames[0] * frame_tokens[0])
    position = jnp.arange(rows, dtype=jnp.int32)
    clip_of = jnp.sum((position[:, None] >= clip_ends[None, :]).astype(jnp.int32), axis=1)
    onehot_clip = (clip_of[:, None] == jnp.arange(slots, dtype=jnp.int32)[None, :]).astype(
        jnp.float32
    )
    modulation = mod_table[0].reshape(1, 3 * width) + jnp.dot(
        onehot_clip, clip_condition[0], precision=HIGH
    )
    shift_rows = modulation[:, :width]
    scale_rows = modulation[:, width : 2 * width]
    gate_rows = modulation[:, 2 * width :]
    inputs_f = tokens_here.astype(jnp.float32)
    centered = inputs_f - jnp.mean(inputs_f, axis=1, keepdims=True)
    inverse = lax.rsqrt(jnp.mean(centered * centered, axis=1, keepdims=True) + EPSILON)
    normed = centered * inverse
    modded = (normed * (1.0 + scale_rows) + shift_rows).astype(jnp.bfloat16)
    tile_onehot = (
        (position // TILE)[:, None] == jnp.arange(tiles, dtype=jnp.int32)[None, :]
    ).astype(jnp.float32)
    live_rows = jnp.dot(tile_onehot, tile_layout[0].astype(jnp.float32), precision=HIGH)
    live_pairs = jnp.dot(live_rows, tile_onehot.T, precision=HIGH) > 0.5
    allowed = live_pairs & (clip_of[:, None] == clip_of[None, :])
    queries = saved[:, :inner].reshape(rows, heads, HEAD)
    key_rows = saved[:, inner : 2 * inner].reshape(rows, heads, HEAD)
    value_rows = saved[:, 2 * inner :].reshape(rows, heads, HEAD)
    factor = HEAD ** (-0.5)
    scores = (
        jnp.einsum("qhd,khd->hqk", queries, key_rows, preferred_element_type=jnp.float32) * factor
    )
    scores = jnp.where(allowed[None], scores, -jnp.inf)
    probs = jax.nn.softmax(scores, axis=2)
    probs_b = probs.astype(jnp.bfloat16)
    attention = (
        jnp.einsum("hqk,khd->qhd", probs_b, value_rows, preferred_element_type=jnp.float32)
        .reshape(rows, inner)
        .astype(jnp.bfloat16)
    )
    out_whole = lax.all_gather(frozen_out[0], "dp", axis=0, tiled=True)
    low_out = jnp.dot(attention, down_out, preferred_element_type=jnp.float32).astype(jnp.bfloat16)
    branch = jnp.dot(attention, out_whole, preferred_element_type=jnp.float32) + contract_last(
        low_out, up_out
    )
    cotangent_f = cotangent[0].astype(jnp.float32)
    gated = (gate_rows * cotangent_f).astype(jnp.bfloat16)
    low_grad_out = jnp.dot(gated, up_out, preferred_element_type=jnp.float32).astype(jnp.bfloat16)
    grad_attention = (
        contract_last(gated, out_whole) + contract_last(low_grad_out, down_out)
    ).astype(jnp.bfloat16)
    grad_heads = grad_attention.reshape(rows, heads, HEAD)
    grad_probs = jnp.einsum(
        "qhd,khd->hqk", grad_heads, value_rows, preferred_element_type=jnp.float32
    )
    delta = jnp.sum(probs * grad_probs, axis=2, keepdims=True)
    grad_scores = (probs * (grad_probs - delta) * factor).astype(jnp.bfloat16)
    grad_query = jnp.einsum(
        "hqk,khd->qhd", grad_scores, key_rows, preferred_element_type=jnp.float32
    ).reshape(rows, inner)
    grad_key = jnp.einsum(
        "hqk,qhd->khd", grad_scores, queries, preferred_element_type=jnp.float32
    ).reshape(rows, inner)
    grad_value = jnp.einsum(
        "hqk,qhd->khd", probs_b, grad_heads, preferred_element_type=jnp.float32
    ).reshape(rows, inner)
    grad_qkv = jnp.concatenate([grad_query, grad_key, grad_value], axis=1).astype(jnp.bfloat16)
    low_in = jnp.dot(modded, down_qkv, preferred_element_type=jnp.float32).astype(jnp.bfloat16)
    low_grad_in = jnp.dot(grad_qkv, up_qkv, preferred_element_type=jnp.float32).astype(jnp.bfloat16)
    frozen_part = contract_last(grad_qkv, lax.all_gather(frozen_qkv[0], "dp", axis=0, tiled=True))
    grad_modded = frozen_part + contract_last(low_grad_in, down_qkv)
    grad_normed = grad_modded * (1.0 + scale_rows)
    grad_input = cotangent_f + inverse * (
        grad_normed
        - jnp.mean(grad_normed, axis=1, keepdims=True)
        - normed * jnp.mean(grad_normed * normed, axis=1, keepdims=True)
    )
    grad_input = grad_input.astype(jnp.bfloat16)
    table_part = jnp.stack(
        [
            jnp.sum(grad_modded, axis=0),
            jnp.sum(grad_modded * normed, axis=0),
            jnp.sum(cotangent_f * branch, axis=0),
        ]
    )
    adapter_part = jnp.concatenate(
        [
            contract_first(modded, low_grad_in),
            contract_first(grad_qkv, low_in),
            contract_first(attention, low_grad_out),
            contract_first(gated, low_out),
        ],
        axis=0,
    )
    replicas = lax.axis_size("dp")
    table_sum = lax.psum(table_part, "dp")
    adapter_sum = lax.psum_scatter(adapter_part, "dp", scatter_dimension=0, tiled=True)
    passed_back = passed_along(grad_input, "pipe", -1)
    return (passed_back[None], (table_sum / replicas)[None], (adapter_sum / replicas)[None])


def solution(mesh):
    placed = (
        P("pipe", "dp", None),
        P("pipe", "dp", None),
        P("pipe", "dp", None),
        P("pipe", None, None),
        P("pipe", "dp", None),
        P("pipe", "dp"),
        P("pipe", "dp"),
        P("pipe", "dp", None),
        P("pipe", "dp", None),
        P("pipe", "dp", None),
        P("pipe", None, None),
    )
    return jax.shard_map(
        on_device,
        mesh=mesh,
        in_specs=placed,
        out_specs=(P("pipe", "dp", None), P("pipe", None, None), P("pipe", "dp", None)),
        check_vma=False,
    )
```

profile of v0, /device:TPU:1, one launch (start us, length us, event | category | flops | bytes accessed | tf_op | source)
XLA Modules:
  0.0 1025.3 jit_solution(3431634579124080414)
XLA Ops:
  7.2 1.5 copy.65
  8.8 1.8 copy.72
  13.9 2.9 copy.62
  18.9 4.2 fusion.93
  23.1 2.3 convolution_convert_fusion
  25.4 1.7 convolution_convert_fusion.3
  27.1 2.0 convolution_add_fusion
  29.5 1.7 convolution_convert_fusion.4
  33.0 114.6 %all-gather.5.cloned.1.call-done = bf16[1,1536,1536]{2,0,1:T(2,128)(2,1)} async-done(((bf16[1,12,1536]{2,0,1:T(2,128)(2,1)}), bf16[1,1536,1536]{2,0,1:T(2,128)(2,1)}) %all-gather.5.cloned.1.call-update) | async-done | bytes 4718608 | tf_op jit(solution)/shard_map/all_gather | solution.py:95
  147.6 5.4 fusion.7
  153.0 2.2 fusion.11
  155.2 2.3 copy.66
  157.5 3.4 fusion.94
  160.9 6.9 fusion.44
  167.9 6.9 fusion.47
  174.8 2.7 convolution_convert_fusion.1
  179.2 154.1 %all-gather.7.cloned.1.call-done = bf16[1,1536,4608]{2,0,1:T(2,128)(2,1)} async-done(((bf16[1,12,4608]{2,0,1:T(2,128)(2,1)}), bf16[1,1536,4608]{2,0,1:T(2,128)(2,1)}) %all-gather.7.cloned.1.call-update) | async-done | bytes 14155792 | tf_op jit(solution)/shard_map/all_gather | solution.py:124
  333.3 14.6 %fusion.2 = f32[256,1536]{1,0:T(8,128)S(1)} fusion(bf16[1,1536,4608]{2,0,1:T(2,128)(2,1)} %all-gather.7.cloned.1.call-done, bf16[256,1536]{0,1:T(8,128)(2,1)} %bitcast.145, bf16[256,1536]{0,1:T(8,128)(2,1)} %bitcast.141, bf16[256,1536]{0,1:T(8,128)(2,1)S(1)} %bitcast.140), kind=kOutput, calls=%fused_computation.2 | convolution fusion | flops 3630956544 | bytes 18087936 | tf_op jit(solution)/shard_map/dot_general | solution.py:21
  347.9 2.4 fusion.91
  350.3 3.6 fusion.35
  353.9 4.3 fusion.58
  358.7 6.9 pad_maximum_fusion
  366.7 5.2 fusion.5
  373.7 642.2 %psum.7 = f32[3,1536]{1,0:T(4,128)S(1)} all-reduce(f32[3,1536]{1,0:T(4,128)S(1)} %pad_maximum_fusion.2), channel_id=1, replica_groups=mesh['dp'=128,'pipe'=2] {'dp'}, use_global_device_ids=true, to_apply=%region_12.13 | all-reduce | flops 4608 | bytes 36864 | tf_op jit(solution)/shard_map/psum | solution.py:150
  (72 shorter events, 15.5 us)
Async XLA Ops:
  7.2 20.0 %copy-start = (f32[1,8,4608]{2,1,0:T(8,128)S(1)}, f32[1,8,4608]{2,1,0:T(8,128)}, u32[]{:S(2)}) copy-start(f32[1,8,4608]{2,1,0:T(8,128)} %param.15) | copy-start | bytes 442372
  7.2 140.4 %all-gather.5.cloned.1.call-start = ((), (), s32[]{:S(2)}) async-start(), calls=%async_computation.1 | async-start | bytes 9510912 | tf_op jit(solution)/shard_map/all_gather | solution.py:95
  8.8 324.5 %all-gather.7.cloned.1.call-start = ((), (), s32[]{:S(2)}) async-start(), calls=%async_computation.2 | async-start | bytes 28532736 | tf_op jit(solution)/shard_map/all_gather | solution.py:124
  10.6 1005.9 %reduce-scatter.4.cloned.1.call-start = ((), (), s32[]{:S(2)}) async-start(), calls=%async_computation.3 | async-start | bytes 4755456
  13.9 2.9 copy-start.3
  18.9 4.2 copy-start.5
  25.4 5.7 copy-start.10
  27.1 2.1 copy-start.4
  29.2 2.3 copy-start.2
  29.5 2.2 copy-start.8
  167.9 6.9 copy-start.7
  174.7 3.6 copy-start.12
  174.7 3.6 copy-start.13
  174.7 3.6 copy-start.15
  177.5 0.9 copy-start.16
  178.3 154.9 %copy-start.14 = (bf16[12,256,128]{1,2,0:T(8,128)(2,1)S(1)}, bf16[12,256,128]{1,2,0:T(8,128)(2,1)}, u32[]{:S(2)}) copy-start(bf16[12,256,128]{1,2,0:T(8,128)(2,1)} %fusion.44) | copy-start | bytes 2359300
  353.9 4.7 copy-start.6
  365.5 1.1 copy-start.11
  366.7 5.2 copy-start.9
  366.7 652.1 %copy-start.1 = (f32[1,8,4608]{2,1,0:T(8,128)S(1)}, f32[1,8,4608]{2,1,0:T(8,128)}, u32[]{:S(2)}) copy-start(f32[1,8,4608]{2,1,0:T(8,128)} %param.15) | copy-start | bytes 442372
  371.9 644.7 %collective-permute-start = (bf16[256,1536]{1,0:T(8,128)(2,1)S(1)}, bf16[256,1536]{1,0:T(8,128)(2,1)S(1)}, u32[]{:S(2)}, u32[]{:S(2)}) collective-permute-start(bf16[256,1536]{1,0:T(8,128)(2,1)S(1)} %copy-done.9), channel_id=1, source_target_pairs={{1,0},{0,1},{3,2},{2,3},{5,4},{4,5},{7,6},{6,7},{9,8},{8,9},{11,10... | collective-permute-start | bytes 2359304 | tf_op jit(solution)/shard_map/ppermute | solution.py:17
Sparse Core Ops, SparseCore 0:
  11.9 135.6 all-gather.4
  151.4 181.7 all-gather.6
  365.7 262.3 reduce-scatter.3
where the time goes:
time: 1030 us
  blocking collectives  642 us (62%)
  waiting for transfers between devices  269 us (26%)
  matrix products  71.6 us (7%)
  other arithmetic  14.4 us (1%)
  between operations  14 us (1%)
  local copies, waits for them, and re-layouts  13.8 us (1%)
    psum x1, blocking collectives, on_device(): table_sum = lax.psum(table_part, 'dp')  642 us
    all_gather x1, waiting for transfers between devices, on_device(): lax.all_gather(frozen_qkv[0], 'dp', axis=0, tiled=True)  154 us
    all_gather x1, waiting for transfers between devices, on_device(): out_whole = lax.all_gather(frozen_out[0], 'dp', axis=0, tiled=True)  115 us
    dot_general x5, matrix products, contract_last(): lax.dot_general(left, right, (((1,), (1,)), ((), ())), preferred_element_...  26.1 us
  transfers between devices with their start and end apart: 4, of which 2 were waited for; matrix products, arithmetic and copies ran while one was open for 6% of the time, Pallas kernels for 0%

commit v1 on v0

--- a/solution.py
+++ b/solution.py
@@ -1,6 +1,10 @@
+import heapq
+
 import jax
 import jax.numpy as jnp
 from jax import lax
+from jax.experimental import pallas as pl
+from jax.experimental.pallas import tpu as pltpu
 from jax.sharding import PartitionSpec as P
 
 HEAD = 128
@@ -27,6 +31,382 @@
     return lax.dot_general(
         left, right, (((0,), (0,)), ((), ())), preferred_element_type=jnp.float32
     )
+
+
+MESH = pl.DeviceIdType.MESH
+NX, NZ, NY, NC = 4, 8, 2, 2
+STEP = {"px": (1, 0), "mx": (3, 0), "pz": (0, 1), "mz": (0, 7)}
+
+
+def spanning_tree(part):
+    edges = {}
+    via_plus = (0, 1, 6) if part == 0 else (2, 7)
+
+    def edge(parent, way):
+        dx, dz = STEP[way]
+        child = ((parent[0] + dx) % NX, (parent[1] + dz) % NZ)
+        edges.setdefault(parent, []).append((way, child))
+
+    edge((0, 0), "pz")
+    edge((0, 0), "mz")
+    edge((0, 1), "pz")
+    edge((0, 7), "mz")
+    for dz in (0, 1, 2, 6, 7):
+        edge((0, dz), "px")
+        edge((0, dz), "mx")
+        if dz in via_plus:
+            edge((1, dz), "px")
+        else:
+            edge((3, dz), "mx")
+    for dx in range(NX):
+        edge((dx, 2), "pz")
+        edge((dx, 6), "mz")
+    for dx in (0, 1):
+        edge((dx, 3), "pz")
+    for dx in (2, 3):
+        edge((dx, 5), "mz")
+    return edges
+
+
+def mirrored(node):
+    return ((-node[0]) % NX, (-node[1]) % NZ)
+
+
+def plan_gather(kinds, lasts, backlog=3.0, latency=1.5, y_time=3.0):
+    trees = [spanning_tree(0), spanning_tree(1)]
+
+    def depth_below(part, node):
+        return max([1 + depth_below(part, c) for _, c in trees[part].get(node, [])], default=0)
+
+    ready = {way: [] for way in STEP}
+    free_at = {way: 0.0 for way in STEP}
+    events = []
+    program = []
+    arrivals = {}
+    count = 0
+
+    def push(kind, part, node):
+        for way, child in trees[part].get(node, []):
+            item = (kind, part, mirrored(node))
+            heapq.heappush(
+                ready[way],
+                (kinds.index(kind), -depth_below(part, node), part, item, child),
+            )
+
+    def serve(now):
+        for way in STEP:
+            while ready[way] and free_at[way] - now < backlog:
+                _, _, _, item, child = heapq.heappop(ready[way])
+                start = max(now, free_at[way])
+                free_at[way] = start + lasts[item[0]]
+                program.append((now, "send", way, item))
+                got = (item[0], item[1], mirrored(child))
+                heapq.heappush(events, (free_at[way] + latency, "recv", way, got, child))
+
+    for kind in kinds:
+        push(kind, 0, (0, 0))
+        heapq.heappush(events, (y_time + 1.5 * kinds.index(kind), "ywait", "", (kind, 1, (0, 0)), (0, 0)))
+    serve(0.0)
+    held = {}
+    while events:
+        now, what, way, item, child = heapq.heappop(events)
+        program.append((now, what, way, item))
+        push(item[0], item[1], child)
+        serve(now)
+        row = (item[0], item[1], item[2][1])
+        held[row] = held.get(row, 0) + 1
+        full = NX - 1 if (item[2][1] == 0 and item[1] == 0) else NX
+        if held[row] == full:
+            program.append((now, "pair", "", row))
+    return program
+
+
+def place():
+    d = lax.axis_index("dp")
+    return d // 64, (d // 16) % 4, (d // 2) % 8, d % 2
+
+
+def at(y, x, z, c):
+    return {"dp": ((y * NX + x) * NZ + z) * NC + c}
+
+
+def greet(others):
+    barrier = pltpu.get_barrier_semaphore()
+    for other in others:
+        pl.semaphore_signal(barrier, inc=1, device_id=other, device_id_type=MESH)
+    pl.semaphore_wait(barrier, len(others))
+
+
+class Gather:
+    def __init__(self, program, bufs, send_sem, recv_sem):
+        self.program, self.bufs = program, bufs
+        self.send_sem, self.recv_sem = send_sem, recv_sem
+        self.ids = {}
+        self.sent = []
+        self.y, self.x, self.z, self.c = place()
+
+    @staticmethod
+    def count(program):
+        return len(Gather.ids_of(program)[0]) , len(Gather.ids_of(program)[1])
+
+    @staticmethod
+    def ids_of(program):
+        recv, send = {}, {}
+        for _, what, way, item in program:
+            if what in ("recv", "ywait", "pair"):
+                recv.setdefault((what, item), len(recv))
+            if what in ("send", "pair"):
+                send.setdefault((what, way, item), len(send))
+            if what == "ywait":
+                send.setdefault((what, way, item), len(send))
+        return recv, send
+
+    def block(self, item):
+        kind, part, (dx, dz) = item
+        y = self.y if part == 0 else 1 - self.y
+        return self.bufs[kind].at[self.c, y, lax.rem(self.x + dx, NX), lax.rem(self.z + dz, NZ)]
+
+    def row(self, item, half):
+        kind, part, dz = item
+        y = self.y if part == 0 else 1 - self.y
+        return self.bufs[kind].at[half, y, :, lax.rem(self.z + dz, NZ)]
+
+    def neighbours(self):
+        y, x, z, c = self.y, self.x, self.z, self.c
+        return {
+            way: at(y, lax.rem(x + dx, NX), lax.rem(z + dz, NZ), c) for way, (dx, dz) in STEP.items()
+        } | {"y": at(1 - y, x, z, c), "pair": at(y, x, z, 1 - c)}
+
+    def start(self):
+        self.recv_id, self.send_id = self.ids_of(self.program)
+        self.near = self.neighbours()
+        self.done = []
+
+    def copy(self, src, dst, send, recv, target):
+        return pltpu.make_async_remote_copy(
+            src_ref=src,
+            dst_ref=dst,
+            send_sem=self.send_sem.at[send],
+            recv_sem=self.recv_sem.at[recv],
+            device_id=target,
+            device_id_type=MESH,
+        )
+
+    def cross(self, kinds):
+        for kind in kinds:
+            own = self.block((kind, 0, (0, 0)))
+            key = ("ywait", (kind, 1, (0, 0)))
+            copy = self.copy(own, own, self.send_id[("ywait", "", key[1])], self.recv_id[key], self.near["y"])
+            copy.start()
+            self.sent.append(copy)
+
+    def step(self, entry):
+        _, what, way, item = entry
+        if what == "send":
+            kind, part, (dx, dz) = item
+            sx, sz = STEP[way]
+            got = (kind, part, ((dx - sx) % NX, (dz - sz) % NZ))
+            ref = self.block(item)
+            copy = self.copy(ref, ref, self.send_id[(what, way, item)], self.recv_id[("recv", got)], self.near[way])
+            copy.start()
+            self.sent.append(copy)
+        elif what in ("recv", "ywait"):
+            ref = self.block(item)
+            self.copy(ref, ref, 0, self.recv_id[(what, item)], self.near["pair"]).wait_recv()
+        elif what == "pair":
+            ref = self.row(item, self.c)
+            copy = self.copy(ref, ref, self.send_id[(what, way, item)], self.recv_id[("pair", item)], self.near["pair"])
+            copy.start()
+            self.sent.append(copy)
+
+    def pair_wait(self, item):
+        ref = self.row(item, 1 - self.c)
+        self.copy(ref, ref, 0, self.recv_id[("pair", item)], self.near["pair"]).wait_recv()
+
+    def finish(self):
+        for copy in self.sent:
+            copy.wait_send()
+
+
+KINDS = ("o", "q")
+PLAN = plan_gather(list(KINDS), {"o": 0.8, "q": 2.4})
+
+
+def gather_kernel(o_in, q_in, wo, wq, send_sem, recv_sem, local_sem):
+    g = Gather(PLAN, {"o": wo, "q": wq}, send_sem, recv_sem)
+    g.start()
+    greet(list(g.near.values()))
+    for i, (kind, ref) in enumerate((("o", o_in), ("q", q_in))):
+        pltpu.make_async_copy(ref, g.block((kind, 0, (0, 0))), local_sem.at[i]).start()
+    for i, (kind, ref) in enumerate((("o", o_in), ("q", q_in))):
+        pltpu.make_async_copy(ref, g.block((kind, 0, (0, 0))), local_sem.at[i]).wait()
+    g.cross(KINDS)
+    for entry in PLAN:
+        g.step(entry)
+    for entry in PLAN:
+        if entry[1] == "pair":
+            g.pair_wait(entry[3])
+    g.finish()
+
+
+def gather_weights(o_in, q_in):
+    recv, send = Gather.ids_of(PLAN)
+    shapes = [
+        jax.ShapeDtypeStruct((NC, NY, NX, NZ) + a.shape, a.dtype) for a in (o_in, q_in)
+    ]
+    return pl.pallas_call(
+        gather_kernel,
+        name="gather_weights",
+        out_shape=shapes,
+        in_specs=[pl.BlockSpec(memory_space=pltpu.VMEM)] * 2,
+        out_specs=[pl.BlockSpec(memory_space=pl.ANY)] * 2,
+        scratch_shapes=[
+            pltpu.SemaphoreType.DMA((len(send),)),
+            pltpu.SemaphoreType.DMA((len(recv),)),
+            pltpu.SemaphoreType.DMA((2,)),
+        ],
+        compiler_params=pltpu.CompilerParams(collective_id=1, has_side_effects=True),
+    )(o_in, q_in)
+
+
+def reduce_kernel(a_ref, t_ref, out_ref, tab_ref, acc, s1, r1, sx, rx, sum2, sz, rz, sy, ry, tx, tz, t2, send_sem, recv_sem):
+    y, x, z, c = place()
+    right, left, across = lax.rem(x + 1, NX), lax.rem(x + 3, NX), lax.rem(x + 2, NX)
+    pair = at(y, x, z, 1 - c)
+    others = [pair, at(1 - y, x, z, c)]
+    others += [at(y, lax.rem(x + i, NX), z, c) for i in range(1, NX)]
+    others += [at(y, x, lax.rem(z + i, NZ), c) for i in range(1, NZ)]
+    greet(others)
+    count = [0]
+    sent = []
+
+    def copy(src, dst, to, here):
+        i = count[0]
+        count[0] += 1
+        out = pltpu.make_async_remote_copy(
+            src_ref=src, dst_ref=dst, send_sem=send_sem.at[i], recv_sem=recv_sem.at[i], device_id=to, device_id_type=MESH
+        )
+        out.start()
+        sent.append(out)
+        return pltpu.make_async_remote_copy(
+            src_ref=src, dst_ref=here, send_sem=send_sem.at[i], recv_sem=recv_sem.at[i], device_id=to, device_id_type=MESH
+        )
+
+    s1[...] = a_ref[:, :, :, 1 - c].astype(jnp.bfloat16)
+    t_pair = copy(t_ref, t2.at[0], pair, t2.at[0])
+    got1 = copy(s1, r1, pair, r1)
+    t_pair.wait_recv()
+    t2[1] = t_ref[...] + t2[0]
+    tx[x] = t2[1]
+    waits = [
+        copy(t2.at[1], tx.at[x], at(y, lax.rem(x + i, NX), z, c), tx.at[lax.rem(x + NX - i, NX)])
+        for i in range(1, NX)
+    ]
+    got1.wait_recv()
+    acc[...] = a_ref[:, :, :, c] + r1[...].astype(jnp.float32)
+    sx[0, 0] = acc[0, across].astype(jnp.bfloat16)
+    sx[1, 0] = acc[1, across].astype(jnp.bfloat16)
+    gp = copy(sx.at[0, 0], rx.at[0, 0], at(y, right, z, c), rx.at[0, 0])
+    gm = copy(sx.at[1, 0], rx.at[1, 0], at(y, left, z, c), rx.at[1, 0])
+    for w in waits:
+        w.wait_recv()
+    t2[2] = ((tx[0] + tx[1]) + tx[2]) + tx[3]
+    tz[z] = t2[2]
+    waits = [
+        copy(t2.at[2], tz.at[z], at(y, x, lax.rem(z + i, NZ), c), tz.at[lax.rem(z + NZ - i, NZ)])
+        for i in range(1, NZ)
+    ]
+    sx[0, 2] = acc[1, right].astype(jnp.bfloat16)
+    sx[1, 2] = acc[0, left].astype(jnp.bfloat16)
+    g2 = [copy(sx.at[0, 2], rx.at[0, 2], at(y, right, z, c), rx.at[0, 2])]
+    g2 += [copy(sx.at[1, 2], rx.at[1, 2], at(y, left, z, c), rx.at[1, 2])]
+    gp.wait_recv()
+    sx[0, 1] = (acc[0, right] + rx[0, 0].astype(jnp.float32)).astype(jnp.bfloat16)
+    g2 += [copy(sx.at[0, 1], rx.at[0, 1], at(y, right, z, c), rx.at[0, 1])]
+    gm.wait_recv()
+    sx[1, 1] = (acc[1, left] + rx[1, 0].astype(jnp.float32)).astype(jnp.bfloat16)
+    g2 += [copy(sx.at[1, 1], rx.at[1, 1], at(y, left, z, c), rx.at[1, 1])]
+    for w in g2:
+        w.wait_recv()
+    sum2[0] = acc[0, x] + rx[0, 1].astype(jnp.float32) + rx[1, 2].astype(jnp.float32)
+    sum2[1] = acc[1, x] + rx[0, 2].astype(jnp.float32) + rx[1, 1].astype(jnp.float32)
+    zwaits = []
+    for i in range(1, NZ):
+        to = lax.rem(z + i, NZ)
+        sz[i, 0] = sum2[0, to].astype(jnp.bfloat16)
+        sz[i, 1] = sum2[1, to].astype(jnp.bfloat16)
+    for i in (1, 7, 2, 6, 3, 5, 4):
+        to = lax.rem(z + i, NZ)
+        zwaits.append(copy(sz.at[i], rz.at[i], at(y, x, to, c), rz.at[i]))
+    for w in waits:
+        w.wait_recv()
+    total = tz[0]
+    for i in range(1, NZ):
+        total = total + tz[i]
+    t2[3] = total
+    ty = copy(t2.at[3], t2.at[4], at(1 - y, x, z, c), t2.at[4])
+    for w in zwaits:
+        w.wait_recv()
+    own = sum2[y, z]
+    far = sum2[1 - y, z]
+    for i in range(1, NZ):
+        own = own + rz[i, y].astype(jnp.float32)
+        far = far + rz[i, 1 - y].astype(jnp.float32)
+    sy[...] = far.astype(jnp.bfloat16)
+    gy = copy(sy, ry, at(1 - y, x, z, c), ry)
+    ty.wait_recv()
+    tab_ref[...] = (t2[3] + t2[4]) * (1.0 / 128)
+    gy.wait_recv()
+    out_ref[...] = (own + ry[...].astype(jnp.float32)) * (1.0 / 128)
+    for s in sent:
+        s.wait_send()
+
+
+def reduce_grads(adapter_part, table_part):
+    rows, rank = adapter_part.shape
+    piece = rows // 128
+    a = adapter_part.reshape(NY, NX, NZ, NC, piece, rank)
+    bf, f32 = jnp.bfloat16, jnp.float32
+    t_shape = (table_part.size // 128, 128)
+    out, tab = pl.pallas_call(
+        reduce_kernel,
+        name="reduce_grads",
+        out_shape=[jax.ShapeDtypeStruct((piece, rank), f32), jax.ShapeDtypeStruct(t_shape, f32)],
+        in_specs=[pl.BlockSpec(memory_space=pltpu.VMEM)] * 2,
+        out_specs=[pl.BlockSpec(memory_space=pltpu.VMEM)] * 2,
+        scratch_shapes=[
+            pltpu.VMEM((NY, NX, NZ, piece, rank), f32),
+            pltpu.VMEM((NY, NX, NZ, piece, rank), bf),
+            pltpu.VMEM((NY, NX, NZ, piece, rank), bf),
+            pltpu.VMEM((2, 3, NZ, piece, rank), bf),
+            pltpu.VMEM((2, 3, NZ, piece, rank), bf),
+            pltpu.VMEM((NY, NZ, piece, rank), f32),
+            pltpu.VMEM((NZ, NY, piece, rank), bf),
+            pltpu.VMEM((NZ, NY, piece, rank), bf),
+            pltpu.VMEM((piece, rank), bf),
+            pltpu.VMEM((piece, rank), bf),
+            pltpu.VMEM((NX,) + t_shape, f32),
+            pltpu.VMEM((NZ,) + t_shape, f32),
+            pltpu.VMEM((5,) + t_shape, f32),
+            pltpu.SemaphoreType.DMA((27,)),
+            pltpu.SemaphoreType.DMA((27,)),
+        ],
+        compiler_params=pltpu.CompilerParams(collective_id=2, has_side_effects=True),
+    )(a, table_part.reshape(t_shape))
+    return out, tab.reshape(table_part.shape)
+
+
+def pair_blocks(frozen_out, frozen_qkv):
+    c = lax.axis_index("dp") % 2
+    route = [(i, i ^ 1) for i in range(lax.axis_size("dp"))]
+    both = []
+    for shard in (frozen_out, frozen_qkv):
+        half = shard.shape[1] // 2
+        low, high = shard[:, :half], shard[:, half:]
+        mine = jnp.where(c == 0, low, high)
+        given = lax.ppermute(jnp.where(c == 0, high, low), "dp", route)
+        both.append(jnp.where(c == 0, jnp.concatenate([mine, given]), jnp.concatenate([given, mine])))
+    return both
 
 
 def on_device(
@@ -92,16 +472,21 @@
         .reshape(rows, inner)
         .astype(jnp.bfloat16)
     )
-    out_whole = lax.all_gather(frozen_out[0], "dp", axis=0, tiled=True)
+    out_pairs, qkv_pairs = pair_blocks(frozen_out[0], frozen_qkv[0])
+    out_halves, qkv_halves = gather_weights(out_pairs, qkv_pairs)
+    out_halves = out_halves.reshape(2, inner, width // 2)
+    qkv_halves = qkv_halves.reshape(2, width, 3 * inner // 2)
     low_out = jnp.dot(attention, down_out, preferred_element_type=jnp.float32).astype(jnp.bfloat16)
-    branch = jnp.dot(attention, out_whole, preferred_element_type=jnp.float32) + contract_last(
-        low_out, up_out
-    )
+    branch = jnp.concatenate(
+        [jnp.dot(attention, half, preferred_element_type=jnp.float32) for half in out_halves], axis=1
+    ) + contract_last(low_out, up_out)
     cotangent_f = cotangent[0].astype(jnp.float32)
     gated = (gate_rows * cotangent_f).astype(jnp.bfloat16)
     low_grad_out = jnp.dot(gated, up_out, preferred_element_type=jnp.float32).astype(jnp.bfloat16)
     grad_attention = (
-        contract_last(gated, out_whole) + contract_last(low_grad_out, down_out)
+        contract_last(gated[:, : width // 2], out_halves[0])
+        + contract_last(gated[:, width // 2 :], out_halves[1])
+        + contract_last(low_grad_out, down_out)
     ).astype(jnp.bfloat16)
     grad_heads = grad_attention.reshape(rows, heads, HEAD)
     grad_probs = jnp.einsum(
@@ -121,8 +506,11 @@
     grad_qkv = jnp.concatenate([grad_query, grad_key, grad_value], axis=1).astype(jnp.bfloat16)
     low_in = jnp.dot(modded, down_qkv, preferred_element_type=jnp.float32).astype(jnp.bfloat16)
     low_grad_in = jnp.dot(grad_qkv, up_qkv, preferred_element_type=jnp.float32).astype(jnp.bfloat16)
-    frozen_part = contract_last(grad_qkv, lax.all_gather(frozen_qkv[0], "dp", axis=0, tiled=True))
-    grad_modded = frozen_part + contract_last(low_grad_in, down_qkv)
+    grad_modded = (
+        contract_last(grad_qkv[:, : 3 * inner // 2], qkv_halves[0])
+        + contract_last(grad_qkv[:, 3 * inner // 2 :], qkv_halves[1])
+        + contract_last(low_grad_in, down_qkv)
+    )
     grad_normed = grad_modded * (1.0 + scale_rows)
     grad_input = cotangent_f + inverse * (
         grad_normed
@@ -146,11 +534,9 @@
         ],
         axis=0,
     )
-    replicas = lax.axis_size("dp")
-    table_sum = lax.psum(table_part, "dp")
-    adapter_sum = lax.psum_scatter(adapter_part, "dp", scatter_dimension=0, tiled=True)
     passed_back = passed_along(grad_input, "pipe", -1)
-    return (passed_back[None], (table_sum / replicas)[None], (adapter_sum / replicas)[None])
+    adapter_mean, table_mean = reduce_grads(adapter_part, table_part)
+    return (passed_back[None], table_mean[None], adapter_mean[None])
 
 
 def solution(mesh):

time: 1030 us -> 202 us (0.20)
  blocking collectives: 642 us -> 0 us
  waiting for transfers between devices: 269 us -> 0.01 us
  Pallas kernels: 0 us -> 102 us
  matrix products: 71.6 us -> 53 us
  between operations: 14 us -> 1.12 us
    psum x1 -> x0, blocking collectives: 642 us -> none  [on_device(): table_sum = lax.psum(table_part, 'dp')]
    all_gather x2 -> x0, waiting for transfers between devices: 269 us -> none  [the longest x1 154 us: on_device(): lax.all_gather(frozen_qkv[0], 'dp', axis=0, tiled=True)]
    pallas_call x0 -> x2, Pallas kernels: none -> 102 us  [the longest x1 69.8 us: gather_weights(): pl.pallas_call(gather_kernel, name='gather_weights', out_shape=shapes, in...]
    dot_general x5 -> x7, matrix products: 26.1 us -> 11.1 us  [contract_last(): lax.dot_general(left, right, (((1,), (1,)), ((), ())), preferred_element_...]
  transfers between devices with their start and end apart: 4 -> 3, of which waited for: 2 -> 0; matrix products, arithmetic and copies ran while one was open for 6% -> 18% of each run, Pallas kernels for 0% -> 16%
where the time goes in v1:
time: 202 us; the launch traced here: 200 us
  Pallas kernels  102 us (50%)
  matrix products  53 us (26%)
  local copies, waits for them, and re-layouts  20.9 us (10%)
  other arithmetic  19.1 us (9%)
  starting transfers between devices  3.64 us (2%)
    pallas_call x1, Pallas kernels, gather_weights(): pl.pallas_call(gather_kernel, name='gather_weights', out_shape=shapes, in...  69.8 us
    pallas_call x1, Pallas kernels, reduce_grads(): pl.pallas_call(reduce_kernel, name='reduce_grads', out_shape=[jax.ShapeDt...  32.6 us
    dot_general x7, matrix products, contract_last(): lax.dot_general(left, right, (((1,), (1,)), ((), ())), preferred_element_...  11.1 us
    dot_general x1, matrix products, on_device(): jnp.einsum('hqk,qhd->khd', grad_scores, queries, preferred_element_type=j...  6.97 us
    concatenate x1, other arithmetic, on_device(): jnp.concatenate([contract_first(modded, low_grad_in), contract_first(grad...  6.87 us
    unnamed x45, local copies, waits for them, and re-layouts  6.74 us
    slice x1, local copies, waits for them, and re-layouts, on_device(): qkv_halves[1]  6.57 us
    dot_general x1, matrix products, on_device(): jnp.einsum('hqk,khd->qhd', grad_scores, key_rows, preferred_element_type=...  6.27 us
  transfers between devices with their start and end apart: 3, of which 0 were waited for; matrix products, arithmetic and copies ran while one was open for 18% of the time, Pallas kernels for 16%

profile of v1, /device:TPU:1, one launch (start us, length us, event | category | flops | bytes accessed | tf_op | source)
XLA Modules:
  0.0 200.2 jit_solution(9290985419342294380)
XLA Ops:
  2.1 3.2 %collective-permute-start = (bf16[12,768]{1,0:T(8,128)(2,1)}, bf16[12,768]{1,0:T(8,128)(2,1)}, u32[]{:S(2)}, u32[]{:S(2)}) collective-permute-start(bf16[12,768]{1,0:T(8,128)(2,1)} %get-tuple-element.36), channel_id=1, source_target_pairs={{0,2},{2,0},{4,6},{6,4},{8,10},{10,8},{12,14},{14,12},{16,18},{18,... | collective-permute-start | bytes 55304 | tf_op jit(solution)/shard_map/ppermute | solution.py:407
  9.1 2.1 %fusion.27 = f32[256]{0:T(256)} fusion(bf16[1,256,1536]{2,1,0:T(8,128)(2,1)} %param.11, f32[256]{0:T(256)S(1)} %broadcast_multiply_fusion.2), kind=kLoop, calls=%fused_computation.37 | loop fusion | flops 1572608 | bytes 788480 | tf_op jit(solution)/shard_map/reduce_sum | solution.py:451
  13.5 3.0 %copy.38 = bf16[1,256,4608]{1,2,0:T(8,128)(2,1)S(1)} copy(bf16[1,256,4608]{2,1,0:T(8,128)(2,1)} %param.12) | data formatting | bytes 4718592 | tf_op args[1]
  17.8 4.2 %fusion.96 = (f32[12,256]{1,0:T(8,128)S(1)}, f32[12,256,256]{1,2,0:T(8,128)}) fusion(pred[256,256]{0,1:T(8,128)(4,1)S(1)} %copy.37, bf16[256,12,128]{0,2,1:T(8,128)(2,1)} %bitcast.142, bf16[256,12,128]{0,2,1:T(8,128)(2,1)} %bitcast.144), kind=kOutput, calls=%fused_computation.127 | convolution fusion | flops 204472576 | bytes 4796416 | tf_op jit(solution)/shard_map/sub | solution.py:468
  22.1 2.3 %convolution_convert_fusion = bf16[12,256,128]{1,2,0:T(8,128)(2,1)S(1)} fusion(bf16[256,12,128]{0,2,1:T(8,128)(2,1)S(1)} %bitcast.138, f32[12,256,256]{1,2,0:T(8,128)} %get-tuple-element.38, f32[12,256]{1,0:T(8,128)S(1)} %get-tuple-element.37), kind=kOutput, calls=%fused_computation.47 | convolution fusion | flops 203292672 | bytes 4730880 | tf_op jit(solution)/shard_map/hqk,khd->qhd/dot_general | solution.py:471
  26.1 2.0 %convolution_add_fusion = f32[256,4608]{1,0:T(8,128)S(1)} fusion(f32[4608]{0:T(1024)S(1)} %add.57, f32[1,8,4608]{2,1,0:T(8,128)S(1)} %copy-done, s32[256]{0:T(256)S(1)} %copy-done.13), kind=kOutput, calls=%fused_computation.2 | convolution fusion | flops 114427904 | bytes 4885504 | tf_op jit(solution)/shard_map/dot_general | solution.py:443
  33.1 69.8 %gather_weights.1 = (bf16[2,2,4,8,24,768]{5,4,3,2,1,0:T(8,128)(2,1)}, bf16[2,2,4,8,24,2304]{5,4,3,2,1,0:T(8,128)(2,1)}) custom-call(bf16[24,768]{1,0:T(8,128)(2,1)} %maximum_select_fusion.1.o_in, bf16[24,2304]{1,0:T(8,128)(2,1)} %maximum_select_fusion.q_in), custom_call_target="tpu_custom_call" | custom-call | tf_op jit(solution)/shard_map/gather_weights/pallas_call | solution.py:257
  102.9 2.8 %fusion.94 = (bf16[1,2,4,8,24,768]{5,4,3,2,1,0:T(8,128)(2,1)S(1)}, bf16[1,2,4,8,24,768]{5,4,3,2,1,0:T(8,128)(2,1)S(1)}) fusion(bf16[2,2,4,8,24,768]{5,4,3,2,1,0:T(8,128)(2,1)} %get-tuple-element.7), kind=kLoop, calls=%fused_computation.125 | loop fusion | bytes 9437184 | tf_op jit(solution)/shard_map/slice | solution.py:488
  105.6 1.7 fusion.101
  108.2 1.7 fusion.102
  110.7 2.3 %fusion.4 = bf16[256,1536]{1,0:T(8,128)(2,1)} fusion(f32[256,1536]{1,0:T(8,128)S(1)} %convolution_add_fusion.4, bf16[256,128]{1,0:T(8,128)(2,1)S(1)} %convolution_convert_fusion.4, bf16[1,9216,128]{2,1,0:T(8,128)(2,1)} %param.21), kind=kOutput, calls=%fused_computation.15 | convolution fusion | flops 101449728 | bytes 2818048 | tf_op jit(solution)/shard_map/dot_general | solution.py:25
  114.4 3.4 %convolution_convert_fusion.1 = bf16[12,128,256]{2,1,0:T(8,128)(2,1)} fusion(bf16[256,12,128]{0,2,1:T(8,128)(2,1)S(1)} %bitcast.140, f32[12,256,256]{1,2,0:T(8,128)} %get-tuple-element.38, f32[12,256]{1,0:T(8,128)S(1)} %copy-done.18), kind=kOutput, calls=%fused_computation.48 | convolution fusion | flops 203292672 | bytes 4730880 | tf_op jit(solution)/shard_map/hqk,qhd->khd/dot_general | solution.py:503
  117.9 2.5 %fusion.97 = f32[12,256,256]{1,2,0:T(8,128)} fusion(bf16[256,12,128]{0,2,1:T(8,128)(2,1)S(1)} %bitcast.141, bf16[256,12,128]{0,2,1:T(8,128)(2,1)S(1)} %bitcast.139), kind=kOutput, calls=%fused_computation.128 | convolution fusion | flops 201326592 | bytes 4718592 | tf_op jit(solution)/shard_map/qhd,khd->hqk/dot_general | solution.py:492
  120.4 6.3 %fusion.35 = bf16[12,256,128]{1,2,0:T(8,128)(2,1)S(1)} fusion(bf16[256,12,128]{0,2,1:T(8,128)(2,1)} %bitcast.145, f32[12,256,256]{1,2,0:T(8,128)} %fusion.97, f32[12,256,256]{1,2,0:T(8,128)} %get-tuple-element.38, f32[12,256]{1,0:T(8,128)S(1)} %copy-done.18), kind=kOutput, calls=%fused_computation.49 | convolution fusion | flops 207228160 | bytes 7876608 | tf_op jit(solution)/shard_map/hqk,khd->qhd/dot_general | solution.py:497
  126.7 7.0 %fusion.38 = bf16[12,256,128]{1,2,0:T(8,128)(2,1)} fusion(bf16[256,12,128]{0,2,1:T(8,128)(2,1)S(1)} %bitcast.143, f32[12,256,256]{1,2,0:T(8,128)} %fusion.97, f32[12,256,256]{1,2,0:T(8,128)} %get-tuple-element.38, f32[12,256]{1,0:T(8,128)S(1)} %copy-done.18), kind=kOutput, calls=%fused_computation.50 | convolution fusion | flops 207228160 | bytes 7876608 | tf_op jit(solution)/shard_map/hqk,qhd->khd/dot_general | solution.py:500
  133.7 6.6 %fusion.93 = (bf16[1,2,4,8,24,2304]{5,4,3,2,1,0:T(8,128)(2,1)S(1)}, bf16[1,2,4,8,24,2304]{5,4,3,2,1,0:T(8,128)(2,1)S(1)}) fusion(bf16[2,2,4,8,24,2304]{5,4,3,2,1,0:T(8,128)(2,1)} %get-tuple-element.8), kind=kLoop, calls=%fused_computation.124 | loop fusion | bytes 28311552 | tf_op jit(solution)/shard_map/slice | solution.py:511
  141.1 2.1 %fusion.44 = f32[256,1536]{1,0:T(8,128)S(1)} fusion(bf16[1536,2304]{1,0:T(8,128)(2,1)S(1)} %bitcast.137, bf16[256,1536]{0,1:T(8,128)(2,1)S(1)} %bitcast.161, bf16[256,1536]{0,1:T(8,128)(2,1)S(1)} %bitcast.157), kind=kOutput, calls=%fused_computation.56 | convolution fusion | flops 1814298624 | bytes 10223616 | tf_op jit(solution)/shard_map/dot_general | solution.py:25
  143.2 2.0 %convolution_add_fusion.5 = f32[256,1536]{1,0:T(8,128)S(1)} fusion(f32[256,1536]{1,0:T(8,128)S(1)} %fusion.44, bf16[1536,2304]{1,0:T(8,128)(2,1)S(1)} %bitcast.136, bf16[256,1536]{0,1:T(8,128)(2,1)S(1)} %bitcast.154, bf16[256,1536]{0,1:T(8,128)(2,1)S(1)} %bitcast.162), kind=kOutput, calls=%fused_computation.14 | convolution fusion | flops 1814691840 | bytes 11796480 | tf_op jit(solution)/shard_map/dot_general | solution.py:25
  146.4 1.7 fusion.25
  148.2 4.0 %fusion.52 = f32[4608,128]{1,0:T(8,128)} fusion(bf16[256,1536]{1,0:T(8,128)(2,1)S(1)} %get-tuple-element.26, bf16[256,1536]{0,1:T(8,128)(2,1)S(1)} %bitcast.155, bf16[256,1536]{0,1:T(8,128)(2,1)} %bitcast.159, bf16[256,1536]{0,1:T(8,128)(2,1)} %bitcast.158, bf16[1,9216,128]{2,1,0:T(8,128)(2,1)} %param.21), kind=kOutput, calls=%fused_computation.66 | convolution fusion | flops 409763840 | bytes 5898240 | tf_op jit(solution)/shard_map/dot_general | solution.py:31
  152.6 2.2 %fusion.42 = f32[1536]{0:T(1024)S(1)} fusion(bf16[256,128]{1,0:T(8,128)(2,1)S(1)} %convolution_convert_fusion.2, f32[256,768]{1,0:T(8,128)} %fusion.102, f32[256,768]{1,0:T(8,128)} %fusion.101, bf16[1,256,1536]{2,1,0:T(8,128)(2,1)} %param.13, bf16[1,9216,128]{2,1,0:T(8,128)(2,1)} %param.21), kind=kOutput, calls=%fused_computation.52 | convolution fusion | flops 102627840 | bytes 2824192 | tf_op jit(solution)/shard_map/dot_general | solution.py:25
  155.9 6.9 %pad_maximum_fusion = f32[9216,128]{1,0:T(8,128)} fusion(f32[1536,128]{1,0:T(8,128)S(1)} %fusion.100, f32[1536,128]{1,0:T(8,128)S(1)} %fusion.99, f32[4608,128]{1,0:T(8,128)} %fusion.52, f32[1536,128]{1,0:T(8,128)S(1)} %fusion.98), kind=kLoop, calls=%fused_computation.3 | loop fusion | flops 3538944 | bytes 9437184 | tf_op jit(solution)/shard_map/concatenate | solution.py:528
  162.8 32.6 %reduce_grads.1 = (f32[72,128]{1,0:T(8,128)}, f32[36,128]{1,0:T(8,128)}) custom-call(f32[2,4,8,2,72,128]{5,4,3,2,1,0:T(8,128)} %bitcast.130, f32[36,128]{1,0:T(8,128)} %reshape.138.t_ref), custom_call_target="tpu_custom_call" | custom-call | tf_op jit(solution)/shard_map/reduce_grads/pallas_call | solution.py:371
  196.7 2.1 %copy.59 = bf16[1,256,1536]{2,1,0:T(8,128)(2,1)} copy(bf16[1,256,1536]{2,1,0:T(8,128)(2,1)} %bitcast.31) | data formatting | bytes 1572864
  (84 shorter events, 24.6 us)
Async XLA Ops:
  0.6 25.5 %copy-start = (f32[1,8,4608]{2,1,0:T(8,128)S(1)}, f32[1,8,4608]{2,1,0:T(8,128)}, u32[]{:S(2)}) copy-start(f32[1,8,4608]{2,1,0:T(8,128)} %param.15) | copy-start | bytes 442372
  2.1 28.8 %collective-permute-start = (bf16[12,768]{1,0:T(8,128)(2,1)}, bf16[12,768]{1,0:T(8,128)(2,1)}, u32[]{:S(2)}, u32[]{:S(2)}) collective-permute-start(bf16[12,768]{1,0:T(8,128)(2,1)} %get-tuple-element.36), channel_id=1, source_target_pairs={{0,2},{2,0},{4,6},{6,4},{8,10},{10,8},{12,14},{14,12},{16,18},{18,... | collective-permute-start | bytes 55304 | tf_op jit(solution)/shard_map/ppermute | solution.py:407
  6.9 25.5 %collective-permute-start.1 = (bf16[12,2304]{1,0:T(8,128)(2,1)}, bf16[12,2304]{1,0:T(8,128)(2,1)S(1)}, u32[]{:S(2)}, u32[]{:S(2)}) collective-permute-start(bf16[12,2304]{1,0:T(8,128)(2,1)} %get-tuple-element.34), channel_id=1, source_target_pairs={{0,2},{2,0},{4,6},{6,4},{8,10},{10,8},{12,14},{14,12},{16,18},{18,... | collective-permute-start | bytes 165896 | tf_op jit(solution)/shard_map/ppermute | solution.py:407
  7.8 5.1 %copy-start.12 = (s32[256]{0:T(256)}, s32[256]{0:T(256)S(1)}, u32[]{:S(2)}) copy-start(s32[256]{0:T(256)S(1)} %convert_reduce_fusion.1) | copy-start | bytes 3076
  22.1 2.3 %copy-start.17 = (f32[12,256]{1,0:T(8,128)}, f32[12,256]{1,0:T(8,128)S(1)}, u32[]{:S(2)}) copy-start(f32[12,256]{1,0:T(8,128)S(1)} %get-tuple-element.37) | copy-start | bytes 36868
  22.1 4.0 %copy-start.13 = (s32[256]{0:T(256)S(1)}, s32[256]{0:T(256)}, u32[]{:S(2)}) copy-start(s32[256]{0:T(256)} %copy-done.12) | copy-start | bytes 3076
  24.4 5.7 %copy-start.8 = (bf16[12,256,128]{1,2,0:T(8,128)(2,1)}, bf16[12,256,128]{1,2,0:T(8,128)(2,1)S(1)}, u32[]{:S(2)}) copy-start(bf16[12,256,128]{1,2,0:T(8,128)(2,1)S(1)} %convolution_convert_fusion) | copy-start | bytes 2359300
  26.1 2.1 %copy-start.4 = (bf16[1,256,1536]{2,1,0:T(8,128)(2,1)S(1)}, bf16[1,256,1536]{2,1,0:T(8,128)(2,1)}, u32[]{:S(2)}) copy-start(bf16[1,256,1536]{2,1,0:T(8,128)(2,1)} %param.13) | copy-start | bytes 2359300
  28.2 2.3 %copy-start.2 = (f32[256,4608]{1,0:T(8,128)}, f32[256,4608]{1,0:T(8,128)S(1)}, u32[]{:S(2)}) copy-start(f32[256,4608]{1,0:T(8,128)S(1)} %convolution_add_fusion) | copy-start | bytes 14155780
  28.4 2.5 %copy-start.11 = (f32[256]{0:T(256)S(1)}, f32[256]{0:T(256)}, u32[]{:S(2)}) copy-start(f32[256]{0:T(256)} %fusion.27) | copy-start | bytes 3076
  102.8 2.8 %copy-start.9 = (bf16[12,256,128]{1,2,0:T(8,128)(2,1)S(1)}, bf16[12,256,128]{1,2,0:T(8,128)(2,1)}, u32[]{:S(2)}) copy-start(bf16[12,256,128]{1,2,0:T(8,128)(2,1)} %copy-done.8) | copy-start | bytes 2359300
  110.7 3.7 %copy-start.18 = (f32[12,256]{1,0:T(8,128)S(1)}, f32[12,256]{1,0:T(8,128)}, u32[]{:S(2)}) copy-start(f32[12,256]{1,0:T(8,128)} %copy-done.17) | copy-start | bytes 36868
  120.4 6.3 %copy-start.6 = (bf16[256,1536]{0,1:T(8,128)(2,1)S(1)}, bf16[256,1536]{0,1:T(8,128)(2,1)}, u32[]{:S(2)}) copy-start(bf16[256,1536]{0,1:T(8,128)(2,1)} %get-tuple-element.32) | copy-start | bytes 2359300
  126.7 14.4 %copy-start.15 = (bf16[12,256,128]{1,2,0:T(8,128)(2,1)}, bf16[12,256,128]{1,2,0:T(8,128)(2,1)S(1)}, u32[]{:S(2)}) copy-start(bf16[12,256,128]{1,2,0:T(8,128)(2,1)S(1)} %fusion.35) | copy-start | bytes 2359300
  133.7 6.6 %copy-start.10 = (bf16[1,9216,128]{2,1,0:T(8,128)(2,1)S(1)}, bf16[1,9216,128]{2,1,0:T(8,128)(2,1)}, u32[]{:S(2)}) copy-start(bf16[1,9216,128]{2,1,0:T(8,128)(2,1)} %param.21) | copy-start | bytes 7077892
  133.7 6.6 %copy-start.14 = (bf16[12,128,256]{2,1,0:T(8,128)(2,1)S(1)}, bf16[12,128,256]{2,1,0:T(8,128)(2,1)}, u32[]{:S(2)}) copy-start(bf16[12,128,256]{2,1,0:T(8,128)(2,1)} %convolution_convert_fusion.1) | copy-start | bytes 2359300
  133.7 6.6 %copy-start.16 = (bf16[12,256,128]{1,2,0:T(8,128)(2,1)S(1)}, bf16[12,256,128]{1,2,0:T(8,128)(2,1)}, u32[]{:S(2)}) copy-start(bf16[12,256,128]{1,2,0:T(8,128)(2,1)} %fusion.38) | copy-start | bytes 2359300
  141.1 4.2 %slice-start = ((s8[4718592]{0:T(1024)(128)(4,1)}), s8[4194304]{0:T(1024)(128)(4,1)S(1)}, s32[]{:S(2)}) async-start(s8[4718592]{0:T(1024)(128)(4,1)} %bitcast.128), calls=%async_computation | async-start | bytes 8388608
  143.2 2.1 %slice-start.1 = ((s8[4718592]{0:T(1024)(128)(4,1)}), s8[524288]{0:T(1024)(128)(4,1)S(1)}, s32[]{:S(2)}) async-start(s8[4718592]{0:T(1024)(128)(4,1)} %bitcast.128), calls=%async_computation.1 | async-start | bytes 1048576
  143.2 2.1 %copy-start.3 = (bf16[1,256,1536]{2,1,0:T(8,128)(2,1)S(1)}, bf16[1,256,1536]{2,1,0:T(8,128)(2,1)}, u32[]{:S(2)}) copy-start(bf16[1,256,1536]{2,1,0:T(8,128)(2,1)} %param.11) | copy-start | bytes 2359300
  145.3 1.1 copy-start.5
  152.6 2.9 %copy-start.7 = (bf16[256,1536]{1,0:T(8,128)(2,1)S(1)}, bf16[256,1536]{1,0:T(8,128)(2,1)}, u32[]{:S(2)}) copy-start(bf16[256,1536]{1,0:T(8,128)(2,1)} %get-tuple-element.27) | copy-start | bytes 2359300
  155.5 41.2 %collective-permute-start.2 = (bf16[256,1536]{1,0:T(8,128)(2,1)S(1)}, bf16[256,1536]{1,0:T(8,128)(2,1)}, u32[]{:S(2)}, u32[]{:S(2)}) collective-permute-start(bf16[256,1536]{1,0:T(8,128)(2,1)S(1)} %copy-done.7), channel_id=1, source_target_pairs={{1,0},{0,1},{3,2},{2,3},{5,4},{4,5},{7,6},{6,7},{9,8},{8,9},{11,10... | collective-permute-start | bytes 2359304 | tf_op jit(solution)/shard_map/ppermute | solution.py:21
  162.8 37.4 %copy-start.1 = (f32[1,8,4608]{2,1,0:T(8,128)S(1)}, f32[1,8,4608]{2,1,0:T(8,128)}, u32[]{:S(2)}) copy-start(f32[1,8,4608]{2,1,0:T(8,128)} %param.15) | copy-start | bytes 442372
